TPU v7x, 32 devices: a whole 2x2x4 slice. The times are simulated.
32 devices in a mesh: dp: 8 (over z, y), tensor: 4 (over x, core).
Axes of the slice: x: 2, y: 2, z: 4, core: 2. Of those that a mesh axis runs over, the one named last changes fastest.
Arguments:
- tokens: bfloat16 [1024, 2048], P('dp'), may hold values from -6 to 6
- cotangent: bfloat16 [1024, 2048], P('dp'), may hold values from -6 to 6
- lengths: int32 [8, 4], P('dp'), may hold values from 1 to 96, 128 in all within a row
- owner_index: int32 [1024], P('dp'), may hold values from 0 to 1023, as said below
- arrival_index: int32 [1024], P('dp'), may hold values from 0 to 1023, as said below
- norm_gain_mixer: float32 [2048], replicated, may hold values from 0.5 to 1.5
- in_weight: bfloat16 [2048, 2, 4096], P(None, None, 'tensor'), may hold values from -0.125 to 0.125
- conv_weight: float32 [4, 4096], P(None, 'tensor'), may hold values from -3 to 3
- conv_bias: float32 [4096], P('tensor'), may hold values from -3 to 3
- xproj_weight: bfloat16 [4096, 160], P('tensor'), may hold values from -0.09375 to 0.09375
- dt_weight: bfloat16 [128, 4096], P(None, 'tensor'), may hold values from -0.5 to 0.5
- dt_bias: float32 [4096], P('tensor'), may hold values from -6.5 to -2.5
- a_log: float32 [16, 4096], P(None, 'tensor'), may hold values from 0 to 2.77
- skip_gain: float32 [4096], P('tensor'), may hold values from 0.5 to 1.5
- out_weight: bfloat16 [4096, 2048], P('tensor'), may hold values from -0.1875 to 0.1875
- norm_gain_mlp: float32 [2048], replicated, may hold values from 0.5 to 1.5
- gate_up_weight: bfloat16 [2048, 2, 8192], P(None, None, 'tensor'), may hold values from -0.125 to 0.125
- down_weight: bfloat16 [8192, 2048], P('tensor'), may hold values from -0.125 to 0.125
Outputs:
- output: bfloat16 [1024, 2048], P('dp')
- tokens_grad: bfloat16 [1024, 2048], P('dp')
- norm_gain_mixer_grad: float32 [2048], P('dp')
- in_weight_grad: float32 [2048, 2, 4096], P('dp', None, 'tensor')
- conv_weight_grad: float32 [4, 4096], P(None, ('tensor', 'dp'))
- conv_bias_grad: float32 [4096], P(('tensor', 'dp'))
- xproj_weight_grad: float32 [4096, 160], P(('tensor', 'dp'))
- dt_weight_grad: float32 [128, 4096], P('dp', 'tensor')
- dt_bias_grad: float32 [4096], P(('tensor', 'dp'))
- a_log_grad: float32 [16, 4096], P(None, ('tensor', 'dp'))
- skip_gain_grad: float32 [4096], P(('tensor', 'dp'))
- out_weight_grad: float32 [4096, 2048], P('tensor', 'dp')
- norm_gain_mlp_grad: float32 [2048], P('dp')
- gate_up_weight_grad: float32 [2048, 2, 8192], P('dp', None, 'tensor')
- down_weight_grad: float32 [8192, 2048], P('tensor', 'dp')
Inputs may be any that keep to these rules, and one draw needn't show every extreme that they name: `owner_index`: A permutation of the 1024 places; the 128 tokens of each index of dp go in exactly 16 to each block of 128 places of the owners' layout. `arrival_index`: the inverse permutation of owner_index. `lengths`: each row sums to 128, and its largest entry is 96.
All inputs are finite; a program needn't handle non-finite values.
Results may differ from a plain program's by a relative error of at most 0.015.
Values may be sent and summed in bfloat16 or wider, within the bound.
A program may use at most 384 MiB of HBM per device.

v0:
```python
import jax
import jax.numpy as jnp
from jax import lax
from jax.sharding import PartitionSpec as P

EPS = 1e-05
highest = lax.Precision.HIGHEST


def rms_scale(values):
    return lax.rsqrt(jnp.mean(values * values, axis=-1, keepdims=True) + EPS)


def rms_back(upstream, values, row_scale):
    return row_scale * (
        upstream
        - values * row_scale * row_scale * jnp.mean(upstream * values, axis=-1, keepdims=True)
    )


def silu_slope(values):
    logistic = jax.nn.sigmoid(values)
    return logistic * (1.0 + values * (1.0 - logistic))


def sequence_offsets(lengths_row, row_count):
    starts = jnp.cumsum(lengths_row) - lengths_row
    positions = jnp.arange(row_count, dtype=jnp.int32)
    begins = jnp.max(jnp.where(starts[None, :] <= positions[:, None], starts[None, :], 0), axis=1)
    return positions - begins


def shift_down(values, amount):
    if amount == 0:
        return values
    padding = jnp.zeros((amount,) + values.shape[1:], values.dtype)
    return jnp.concatenate([padding, values[:-amount]], axis=0)


def shift_up(values, amount):
    if amount == 0:
        return values
    padding = jnp.zeros((amount,) + values.shape[1:], values.dtype)
    return jnp.concatenate([values[amount:], padding], axis=0)


def causal_conv(inner_part, weight, conv_bias, offset):
    conv_taps = weight.shape[0]
    summed = conv_bias[None, :] + weight[conv_taps - 1][None, :] * inner_part
    for distance in range(1, conv_taps):
        valid_rows = (offset >= distance).astype(jnp.float32)[:, None]
        summed = (
            summed
            + weight[conv_taps - 1 - distance][None, :]
            * shift_down(inner_part, distance)
            * valid_rows
        )
    return summed


def combine(first_pair, second_pair):
    return (first_pair[0] * second_pair[0], second_pair[0] * first_pair[1] + second_pair[1])


def decay_factor(step_size, keep_mask, decay_rate):
    return jnp.exp(step_size[:, None, :] * decay_rate[None, :, :]) * keep_mask[:, None, None]


def to_blocks(values, block_count):
    return values.reshape((block_count, values.shape[0] // block_count) + values.shape[1:])


def scan_forward(step_size, b_proj, c_proj, conv_in, keep_mask, decay_rate):
    row_count = step_size.shape[0]
    block_count = row_count // min(64, row_count)

    def advance(carried, pieces):
        block_step, block_b, block_c, block_conv, block_keep = pieces
        factor = decay_factor(block_step, block_keep, decay_rate)
        source = block_step[:, None, :] * block_b[:, :, None] * block_conv[:, None, :]
        cumulative, partial_state = lax.associative_scan(combine, (factor, source), axis=0)
        states = cumulative * carried[None] + partial_state
        result = jnp.einsum("tn,tnc->tc", block_c, states, precision=highest)
        return (states[-1], (states, result))

    initial = jnp.zeros(decay_rate.shape, jnp.float32)
    pieces = tuple(
        (
            to_blocks(values, block_count)
            for values in (step_size, b_proj, c_proj, conv_in, keep_mask)
        )
    )
    final_state, (states, results) = lax.scan(advance, initial, pieces)
    return (states.reshape((row_count,) + decay_rate.shape), results.reshape(row_count, -1))


def scan_backward(states_all, step_size, b_proj, c_proj, conv_in, keep_mask, decay_rate, d_scanned):
    row_count = step_size.shape[0]
    block_count = row_count // min(64, row_count)
    previous_all = shift_down(states_all, 1)

    def retreat(carry, pieces):
        incoming, decay_grad = carry
        states, previous, block_step, block_b, block_c, block_conv, block_keep, block_grad = pieces
        factor = decay_factor(block_step, block_keep, decay_rate)
        emitted = block_c[:, :, None] * block_grad[:, None, :]
        following = jnp.concatenate([factor[1:], jnp.ones_like(factor[:1])], axis=0)
        reach, local_grad = lax.associative_scan(
            combine, (jnp.flip(following, 0), jnp.flip(emitted, 0)), axis=0
        )
        state_grad = jnp.flip(local_grad, 0) + jnp.flip(reach, 0) * incoming[None]
        via_factor = state_grad * previous * factor
        b_weighted = jnp.einsum("tnc,tn->tc", state_grad, block_b, precision=highest)
        step_grad = (
            jnp.einsum("tnc,nc->tc", via_factor, decay_rate, precision=highest)
            + block_conv * b_weighted
        )
        b_grad = jnp.einsum("tnc,tc->tn", state_grad, block_step * block_conv, precision=highest)
        c_grad = jnp.einsum("tc,tnc->tn", block_grad, states, precision=highest)
        conv_grad = block_step * b_weighted
        decay_grad = decay_grad + jnp.einsum(
            "tnc,tc->nc", via_factor, block_step, precision=highest
        )
        return ((factor[0] * state_grad[0], decay_grad), (step_grad, b_grad, c_grad, conv_grad))

    zero_state = jnp.zeros(decay_rate.shape, jnp.float32)
    pieces = tuple(
        (
            to_blocks(values, block_count)
            for values in (
                states_all,
                previous_all,
                step_size,
                b_proj,
                c_proj,
                conv_in,
                keep_mask,
                d_scanned,
            )
        )
    )
    (leftover, decay_grad), block_grads = lax.scan(
        retreat, (zero_state, zero_state), pieces, reverse=True
    )
    return (
        decay_grad,
        tuple((stacked.reshape((row_count,) + stacked.shape[2:]) for stacked in block_grads)),
    )


def body(
    tokens,
    cotangent,
    lengths,
    owner_index,
    arrival_index,
    norm_gain_mixer,
    in_weight,
    conv_weight,
    conv_bias,
    xproj_weight,
    dt_weight,
    dt_bias,
    a_log,
    skip_gain,
    out_weight,
    norm_gain_mlp,
    gate_up_weight,
    down_weight,
):
    row_count = tokens.shape[0]
    model_width = tokens.shape[1]
    inner_width = in_weight.shape[2]
    hidden_width = gate_up_weight.shape[2]
    rank_width = dt_weight.shape[0]
    state_width = a_log.shape[0]
    positions = jnp.arange(row_count, dtype=jnp.int32)
    send_order = jnp.argsort(owner_index)
    arrived = (
        lax.all_to_all(tokens[send_order], "dp", split_axis=0, concat_axis=0, tiled=True),
        lax.all_to_all(cotangent[send_order], "dp", split_axis=0, concat_axis=0, tiled=True),
    )
    slot_order = jnp.argsort(arrival_index // row_count * row_count + positions)
    slot_rank = jnp.argsort(slot_order)
    owned_rows = arrived[0][slot_rank].astype(jnp.float32)
    owned_grad = arrived[1][slot_rank]
    offset = sequence_offsets(lengths[0], row_count)
    keep_mask = (offset > 0).astype(jnp.float32)
    scale_mixer = rms_scale(owned_rows)
    normed = (owned_rows * scale_mixer * norm_gain_mixer).astype(jnp.bfloat16)
    in_flat = in_weight.reshape(model_width, 2 * inner_width)
    projected = jnp.dot(normed, in_flat, preferred_element_type=jnp.float32)
    inner_part = projected[:, :inner_width]
    gate_z = projected[:, inner_width:]
    conv_pre = causal_conv(inner_part, conv_weight, conv_bias, offset)
    conv_out = jax.nn.silu(conv_pre).astype(jnp.bfloat16)
    conv_in = conv_out.astype(jnp.float32)
    pieces = lax.psum(jnp.dot(conv_out, xproj_weight, preferred_element_type=jnp.float32), "tensor")
    dt_low = pieces[:, :rank_width].astype(jnp.bfloat16)
    b_proj = pieces[:, rank_width : rank_width + state_width]
    c_proj = pieces[:, rank_width + state_width :]
    dt_pre = jnp.dot(dt_low, dt_weight, preferred_element_type=jnp.float32) + dt_bias
    step_size = jax.nn.softplus(dt_pre)
    decay_rate = -jnp.exp(a_log)
    states_all, scan_part = scan_forward(step_size, b_proj, c_proj, conv_in, keep_mask, decay_rate)
    scanned = scan_part + skip_gain * conv_in
    silu_z = jax.nn.silu(gate_z)
    gated = (scanned * silu_z).astype(jnp.bfloat16)
    mixer_out = lax.psum(jnp.dot(gated, out_weight, preferred_element_type=jnp.float32), "tensor")
    hidden_in = owned_rows + mixer_out
    scale_mlp = rms_scale(hidden_in)
    normed_mlp = (hidden_in * scale_mlp * norm_gain_mlp).astype(jnp.bfloat16)
    gate_flat = gate_up_weight.reshape(model_width, 2 * hidden_width)
    gate_up = jnp.dot(normed_mlp, gate_flat, preferred_element_type=jnp.float32)
    gate_part = gate_up[:, :hidden_width]
    up_part = gate_up[:, hidden_width:]
    hidden = (jax.nn.silu(gate_part) * up_part).astype(jnp.bfloat16)
    down_out = lax.psum(jnp.dot(hidden, down_weight, preferred_element_type=jnp.float32), "tensor")
    output_own = (hidden_in + down_out).astype(jnp.bfloat16)
    upstream = owned_grad.astype(jnp.float32)
    d_hidden = jnp.einsum("td,fd->tf", owned_grad, down_weight, preferred_element_type=jnp.float32)
    down_grad = jnp.einsum("tf,td->fd", hidden, owned_grad, preferred_element_type=jnp.float32)
    d_gate = d_hidden * up_part * silu_slope(gate_part)
    d_up = d_hidden * jax.nn.silu(gate_part)
    d_gate_up = jnp.concatenate([d_gate, d_up], axis=1).astype(jnp.bfloat16)
    gate_up_grad = jnp.einsum(
        "td,tk->dk", normed_mlp, d_gate_up, preferred_element_type=jnp.float32
    ).reshape(model_width, 2, hidden_width)
    d_normed_mlp = lax.psum(
        jnp.einsum("tk,dk->td", d_gate_up, gate_flat, preferred_element_type=jnp.float32), "tensor"
    )
    gain_mlp_grad = jnp.sum(d_normed_mlp * hidden_in * scale_mlp, axis=0)
    d_hidden_in = upstream + rms_back(d_normed_mlp * norm_gain_mlp, hidden_in, scale_mlp)
    d_mixed = d_hidden_in.astype(jnp.bfloat16)
    d_gated = jnp.einsum("td,cd->tc", d_mixed, out_weight, preferred_element_type=jnp.float32)
    out_grad = jnp.einsum("tc,td->cd", gated, d_mixed, preferred_element_type=jnp.float32)
    d_scanned = d_gated * silu_z
    d_gate_z = d_gated * scanned * silu_slope(gate_z)
    skip_grad = jnp.sum(d_scanned * conv_in, axis=0)
    decay_grad, (d_step, d_b_proj, d_c_proj, d_conv_scan) = scan_backward(
        states_all, step_size, b_proj, c_proj, conv_in, keep_mask, decay_rate, d_scanned
    )
    a_log_grad = decay_grad * decay_rate
    d_dt_pre = d_step * jax.nn.sigmoid(dt_pre)
    dt_bias_grad = jnp.sum(d_dt_pre, axis=0)
    d_dt_rounded = d_dt_pre.astype(jnp.bfloat16)
    dt_weight_grad = jnp.einsum(
        "tr,tc->rc", dt_low, d_dt_rounded, preferred_element_type=jnp.float32
    )
    d_dt_low = jnp.einsum("tc,rc->tr", d_dt_rounded, dt_weight, preferred_element_type=jnp.float32)
    d_pieces = lax.psum(jnp.concatenate([d_dt_low, d_b_proj, d_c_proj], axis=1), "tensor").astype(
        jnp.bfloat16
    )
    xproj_grad = jnp.einsum("tc,tk->ck", conv_out, d_pieces, preferred_element_type=jnp.float32)
    d_conv = (
        d_scanned * skip_gain
        + d_conv_scan
        + jnp.einsum("tk,ck->tc", d_pieces, xproj_weight, preferred_element_type=jnp.float32)
    )
    d_conv_pre = d_conv * silu_slope(conv_pre)
    conv_bias_grad = jnp.sum(d_conv_pre, axis=0)
    conv_taps = conv_weight.shape[0]
    tap_grads = []
    d_inner = jnp.zeros_like(inner_part)
    for distance in range(conv_taps):
        valid_grad = d_conv_pre * (offset >= distance).astype(jnp.float32)[:, None]
        tap_grads.append(jnp.sum(valid_grad * shift_down(inner_part, distance), axis=0))
        d_inner = d_inner + conv_weight[conv_taps - 1 - distance][None, :] * shift_up(
            valid_grad, distance
        )
    conv_weight_grad = jnp.stack(tap_grads[::-1], axis=0)
    d_projected = jnp.concatenate([d_inner, d_gate_z], axis=1).astype(jnp.bfloat16)
    in_grad = jnp.einsum(
        "td,tk->dk", normed, d_projected, preferred_element_type=jnp.float32
    ).reshape(model_width, 2, inner_width)
    d_normed = lax.psum(
        jnp.einsum("tk,dk->td", d_projected, in_flat, preferred_element_type=jnp.float32), "tensor"
    )
    gain_mixer_grad = jnp.sum(d_normed * owned_rows * scale_mixer, axis=0)
    d_tokens = d_hidden_in + rms_back(d_normed * norm_gain_mixer, owned_rows, scale_mixer)
    back_order = jnp.argsort(arrival_index)
    returned = (
        lax.all_to_all(output_own[back_order], "dp", split_axis=0, concat_axis=0, tiled=True),
        lax.all_to_all(
            d_tokens.astype(jnp.bfloat16)[back_order], "dp", split_axis=0, concat_axis=0, tiled=True
        ),
    )
    arrive_order = jnp.argsort(owner_index // row_count * row_count + positions)
    arrive_rank = jnp.argsort(arrive_order)
    output = returned[0][arrive_rank]
    tokens_grad = returned[1][arrive_rank]
    summed = (
        lax.psum_scatter(gain_mixer_grad, "dp", scatter_dimension=0, tiled=True),
        lax.psum_scatter(in_grad, "dp", scatter_dimension=0, tiled=True),
        lax.psum_scatter(conv_weight_grad, "dp", scatter_dimension=1, tiled=True),
        lax.psum_scatter(conv_bias_grad, "dp", scatter_dimension=0, tiled=True),
        lax.psum_scatter(xproj_grad, "dp", scatter_dimension=0, tiled=True),
        lax.psum_scatter(dt_weight_grad, "dp", scatter_dimension=0, tiled=True),
        lax.psum_scatter(dt_bias_grad, "dp", scatter_dimension=0, tiled=True),
        lax.psum_scatter(a_log_grad, "dp", scatter_dimension=1, tiled=True),
        lax.psum_scatter(skip_grad, "dp", scatter_dimension=0, tiled=True),
        lax.psum_scatter(out_grad, "dp", scatter_dimension=1, tiled=True),
        lax.psum_scatter(gain_mlp_grad, "dp", scatter_dimension=0, tiled=True),
        lax.psum_scatter(gate_up_grad, "dp", scatter_dimension=0, tiled=True),
        lax.psum_scatter(down_grad, "dp", scatter_dimension=1, tiled=True),
    )
    return (
        output,
        tokens_grad,
        summed[0],
        summed[1],
        summed[2],
        summed[3],
        summed[4],
        summed[5],
        summed[6],
        summed[7],
        summed[8],
        summed[9],
        summed[10],
        summed[11],
        summed[12],
    )


def solution(mesh):
    in_specs = (
        P("dp", None),
        P("dp", None),
        P("dp", None),
        P("dp"),
        P("dp"),
        P(),
        P(None, None, "tensor"),
        P(None, "tensor"),
        P("tensor"),
        P("tensor", None),
        P(None, "tensor"),
        P("tensor"),
        P(None, "tensor"),
        P("tensor"),
        P("tensor", None),
        P(),
        P(None, None, "tensor"),
        P("tensor", None),
    )
    out_specs = (
        P("dp", None),
        P("dp", None),
        P("dp"),
        P("dp", None, "tensor"),
        P(None, ("tensor", "dp")),
        P(("tensor", "dp")),
        P(("tensor", "dp"), None),
        P("dp", "tensor"),
        P(("tensor", "dp")),
        P(None, ("tensor", "dp")),
        P(("tensor", "dp")),
        P("tensor", "dp"),
        P("dp"),
        P("dp", None, "tensor"),
        P("tensor", "dp"),
    )
    return jax.shard_map(body, mesh=mesh, in_specs=in_specs, out_specs=out_specs, check_vma=False)
```

profile of v0, /device:TPU:0, one launch (start us, length us, event | category | flops | bytes accessed | tf_op | source)
XLA Modules:
  0.0 3473.5 jit_solution(9165166112608574943)
XLA Ops:
  19.8 10.3 copy.114
  54.3 29.8 all-reduce.73.cloned.1.call-done
  89.1 443.6 %while.39 = (s32[]{:T(128)}, f32[16,1024]{1,0:T(8,128)}, f32[2,64,16,1024]{3,2,1,0:T(8,128)}, f32[2,64,1024]{2,1,0:T(8,128)}, f32[2,64,1024]{2,1,0:T(8,128)S(1)}...) while((s32[]{:T(128)}, f32[16,1024]{1,0:T(8,128)}, ...), condition=%wide.region_8.9_spmd, body=%wide.region_7.8_spmd.sunk | while | flops 32800768 | bytes 281060864 | solution.py:93
  160.8 10.2 pad.626
  187.0 10.2 pad.628
  206.2 18.7 pad.629
  229.0 18.5 pad.630
  251.4 18.5 pad.631
  273.3 18.6 pad.632
  291.9 10.5 bitcast_dynamic-update-slice_fusion.7
  382.4 10.2 pad.626
  408.6 10.2 pad.628
  427.9 18.7 pad.629
  450.6 18.5 pad.630
  473.1 18.5 pad.631
  494.9 18.6 pad.632
  513.5 10.4 bitcast_dynamic-update-slice_fusion.7
  538.9 17.3 copy.115
  590.7 12.9 fusion.46
  609.8 30.4 all-reduce.77.cloned.1.call-done
  652.3 533.0 %while.40 = (s32[]{:T(128)}, f32[16,1024]{1,0:T(8,128)}, f32[16,1024]{1,0:T(8,128)}, f32[2,64,1024]{2,1,0:T(8,128)}, f32[2,64,16]{1,0,2:T(2,128)}, /*index=5*/f3...) while((s32[]{:T(128)}, f32[16,1024]{1,0:T(8,128)}, ...), condition=%wide.region_18.19_spmd.clone, body=%wide.region_17.18_spmd.clone.sunk | while | flops 69206016 | bytes 426660448 | solution.py:142
  736.2 10.2 pad.668
  753.9 10.2 pad.669
  767.2 10.2 pad.670
  785.8 18.6 pad.671
  808.5 18.7 pad.672
  835.6 18.5 pad.673
  857.4 18.7 pad.674
  998.4 10.2 pad.668
  1016.1 10.2 pad.669
  1029.4 10.2 pad.670
  1048.0 18.6 pad.671
  1070.7 18.7 pad.672
  1097.8 18.5 pad.673
  1119.6 18.7 pad.674
  1190.7 11.6 psum.46
  1220.2 25.6 copy.63
  1247.3 13.4 fusion.45
  1260.7 42.7 %reshape.191 = f32[2048,2,2048]{2,1,0:T(2,128)} reshape(f32[2048,4096]{1,0:T(8,128)} %fusion.45) | data formatting | bytes 67108864 | tf_op jit(solution)/shard_map/reshape | solution.py:228
  1339.4 23.2 all-to-all-done.1
  1377.3 46.1 %all-reduce.64 = (f32[2048]{0:T(1024)S(1)}, f32[1024]{0:T(1024)S(1)}, f32[1024]{0:T(1024)S(1)}, f32[1024]{0:T(1024)S(1)}, f32[2048]{0:T(1024)S(1)}) all-reduce(f32[2048]{0:T(1024)S(1)} %get-tuple-element.560, f32[1024]{0:T(1024)S(1)} %get-tuple-element.562, ...), channel_id=2, replica_groups=mesh['dp'=8,'tensor'=4] {'dp'}, use_global_device_ids=true, to_apply=%region_23.24.clone | all-reduce | flops 7168 | bytes 57344
  1429.9 431.9 %all-reduce.79.cloned.1.call-done = f32[2048,2,1024]{2,1,0:T(2,128)} async-done(((f32[2048,2,1024]{2,1,0:T(2,128)}), f32[2048,2,1024]{2,1,0:T(2,128)}) %all-reduce.79.cloned.1.call-update) | async-done | bytes 16777232
  1865.5 974.2 %all-reduce.81.cloned.1.call-done = f32[2048,2,2048]{2,1,0:T(2,128)} async-done(((f32[2048,2,2048]{2,1,0:T(2,128)}), f32[2048,2,2048]{2,1,0:T(2,128)}) %all-reduce.81.cloned.1.call-update) | async-done | bytes 33554448
  2845.8 50.7 %reduce-scatter.13.cloned.1.call-done = f32[16,128]{1,0:T(8,128)} async-done(((f32[16,1024]{1,0:T(8,128)}), f32[16,128]{1,0:T(8,128)}) %reduce-scatter.13.cloned.1.call-update) | async-done | bytes 8208 | tf_op jit(solution)/shard_map/reduce_scatter | solution.py:300
  2896.5 65.3 %reduce-scatter.11.cloned.1.call-done = f32[16,1024]{1,0:T(8,128)} async-done(((f32[128,1024]{1,0:T(8,128)}), f32[16,1024]{1,0:T(8,128)}) %reduce-scatter.11.cloned.1.call-update) | async-done | bytes 65552 | tf_op jit(solution)/shard_map/reduce_scatter | solution.py:298
  2961.7 65.5 %reduce-scatter.9.cloned.1.call-done = f32[128,160]{0,1:T(8,128)} async-done(((f32[1024,160]{0,1:T(8,128)}), f32[128,160]{0,1:T(8,128)}) %reduce-scatter.9.cloned.1.call-update) | async-done | bytes 81936 | tf_op jit(solution)/shard_map/reduce_scatter | solution.py:297
  3027.2 153.2 %reduce-scatter.15.cloned.1.call-done = f32[1024,256]{1,0:T(8,128)} async-done(((f32[1024,2048]{1,0:T(8,128)}), f32[1024,256]{1,0:T(8,128)}) %reduce-scatter.15.cloned.1.call-update) | async-done | bytes 1048592 | tf_op jit(solution)/shard_map/reduce_scatter | solution.py:302
  3180.4 286.0 %reduce-scatter.17.cloned.1.call-done = f32[2048,256]{1,0:T(8,128)} async-done(((f32[2048,2048]{1,0:T(8,128)}), f32[2048,256]{1,0:T(8,128)}) %reduce-scatter.17.cloned.1.call-update) | async-done | bytes 2097168 | tf_op jit(solution)/shard_map/reduce_scatter | solution.py:305
  (786 shorter events, 736.7 us)
Async XLA Ops:
  12.2 25.5 all-to-all-start
  37.7 518.5 %all-to-all-start.2 = ((bf16[8,16,2048]{2,1,0:T(8,128)(2,1)}), bf16[8,16,2048]{2,1,0:T(8,128)(2,1)}, u32[]{:S(2)}, u32[]{:S(2)}) async-start(bf16[8,16,2048]{2,1,0:T(8,128)(2,1)} %bitcast.26), calls=%async_computation.2 | async-start | bytes 1048576 | tf_op jit(solution)/shard_map/all_to_all | solution.py:181
  43.7 40.4 %all-reduce.73.cloned.1.call-start = ((), (), s32[]{:S(2)}) async-start(), calls=%async_computation.10 | async-start | bytes 163840 | tf_op jit(solution)/shard_map/psum | solution.py:198
  49.6 38.0 %copy-start.42 = (f32[128,2048]{1,0:T(8,128)}, f32[128,2048]{1,0:T(8,128)S(1)}, u32[]{:S(2)}) copy-start(f32[128,2048]{1,0:T(8,128)S(1)} %fusion.55) | copy-start | bytes 3145732
  49.6 35.9 %copy-start.82 = (bf16[128,1024]{1,0:T(8,128)(2,1)S(1)}, bf16[128,1024]{1,0:T(8,128)(2,1)}, u32[]{:S(2)}) copy-start(bf16[128,1024]{1,0:T(8,128)(2,1)} %param.32) | copy-start | bytes 786436
  49.7 35.9 %copy-start.114 = (f32[1024]{0:T(1024)S(1)}, f32[1024]{0:T(1024)}, u32[]{:S(2)}) copy-start(f32[1024]{0:T(1024)} %param.33) | copy-start | bytes 12292
  49.7 39.4 %copy-start.58 = (f32[125,1024]{1,0:T(8,128)}, f32[125,1024]{1,0:T(8,128)S(1)}, u32[]{:S(2)}) copy-start(f32[125,1024]{1,0:T(8,128)S(1)} %slice.947) | copy-start | bytes 1536004
  49.8 39.4 %copy-start.59 = (f32[126,1024]{1,0:T(8,128)}, f32[126,1024]{1,0:T(8,128)S(1)}, u32[]{:S(2)}) copy-start(f32[126,1024]{1,0:T(8,128)S(1)} %slice.946) | copy-start | bytes 1548292
  51.9 33.0 copy-start.53
  52.8 523.8 %all-reduce.75.cloned.1.call-start = ((), (), s32[]{:S(2)}) async-start(), calls=%async_computation.11 | async-start | bytes 2097152 | tf_op jit(solution)/shard_map/psum | solution.py:209
  96.1 29.0 copy-start.22
  97.7 19.3 copy-start.27
  273.3 18.6 copy-start.67
  317.7 29.0 copy-start.22
  319.3 19.3 copy-start.27
  494.9 18.6 copy-start.67
  538.8 101.5 %all-reduce.77.cloned.1.call-start = ((), (), s32[]{:S(2)}) async-start(), calls=%async_computation.12 | async-start | bytes 2097152 | tf_op jit(solution)/shard_map/psum | solution.py:229
  558.9 83.7 %copy-start.56 = (bf16[128,2048]{1,0:T(8,128)(2,1)}, bf16[128,2048]{1,0:T(8,128)(2,1)S(1)}, u32[]{:S(2)}) copy-start(bf16[128,2048]{1,0:T(8,128)(2,1)S(1)} %gather_fusion.5) | copy-start | bytes 1572868
  563.3 14.9 copy-start.83
  578.2 64.4 %copy-start.35 = (f32[128,2048]{1,0:T(8,128)}, f32[128,2048]{1,0:T(8,128)S(1)}, u32[]{:S(2)}) copy-start(f32[128,2048]{1,0:T(8,128)S(1)} %get-tuple-element.638) | copy-start | bytes 3145732
  578.2 64.4 %copy-start.105 = (f32[128]{0:T(128)}, f32[128]{0:T(128)S(1)}, u32[]{:S(2)}) copy-start(f32[128]{0:T(128)S(1)} %add_rsqrt_fusion) | copy-start | bytes 1540
  603.6 723.3 %all-reduce.83.cloned.1.call-start = ((), (), s32[]{:S(2)}) async-start(), calls=%async_computation.21 | async-start | bytes 4194304 | tf_op jit(solution)/shard_map/psum | solution.py:218
  609.8 34.3 copy-start.43
  609.8 34.3 copy-start.54
  609.8 34.3 copy-start.107
  665.4 35.1 %copy-start.23 = (f32[16,16,1024]{2,1,0:T(8,128)}, f32[16,16,1024]{2,1,0:T(8,128)S(1)}, u32[]{:S(2)}) copy-start(f32[16,16,1024]{2,1,0:T(8,128)S(1)} %get-tuple-element.999) | copy-start | bytes 3145732 | tf_op jit(solution)/shard_map/while
  667.0 20.7 copy-start.28
  898.7 15.3 copy-start.69
  899.7 14.3 copy-start.92
  927.7 35.1 %copy-start.23 = (f32[16,16,1024]{2,1,0:T(8,128)}, f32[16,16,1024]{2,1,0:T(8,128)S(1)}, u32[]{:S(2)}) copy-start(f32[16,16,1024]{2,1,0:T(8,128)S(1)} %get-tuple-element.999) | copy-start | bytes 3145732 | tf_op jit(solution)/shard_map/while
  929.2 20.7 copy-start.28
  1160.9 15.3 copy-start.69
  1161.9 14.3 copy-start.92
  1210.6 165.2 %reduce-scatter.19.cloned.1.call-start = ((), (), s32[]{:S(2)}) async-start(), calls=%async_computation.18 | async-start | bytes 589824
  1211.7 650.1 %all-reduce.79.cloned.1.call-start = ((), (), s32[]{:S(2)}) async-start(), calls=%async_computation.19 | async-start | bytes 33554432
  1245.8 1593.9 %all-reduce.81.cloned.1.call-start = ((), (), s32[]{:S(2)}) async-start(), calls=%async_computation.20 | async-start | bytes 67108864
  1303.4 1593.0 %reduce-scatter.13.cloned.1.call-start = ((), (), s32[]{:S(2)}) async-start(), calls=%async_computation.15 | async-start | bytes 73728 | tf_op jit(solution)/shard_map/reduce_scatter | solution.py:300
  1305.7 1656.0 %reduce-scatter.11.cloned.1.call-start = ((), (), s32[]{:S(2)}) async-start(), calls=%async_computation.14 | async-start | bytes 589824 | tf_op jit(solution)/shard_map/reduce_scatter | solution.py:298
  1307.7 1719.5 %reduce-scatter.9.cloned.1.call-start = ((), (), s32[]{:S(2)}) async-start(), calls=%async_computation.13 | async-start | bytes 737280 | tf_op jit(solution)/shard_map/reduce_scatter | solution.py:297
  1308.9 1871.6 %reduce-scatter.15.cloned.1.call-start = ((), (), s32[]{:S(2)}) async-start(), calls=%async_computation.16 | async-start | bytes 9437184 | tf_op jit(solution)/shard_map/reduce_scatter | solution.py:302
  1313.6 2152.9 %reduce-scatter.17.cloned.1.call-start = ((), (), s32[]{:S(2)}) async-start(), calls=%async_computation.17 | async-start | bytes 18874368 | tf_op jit(solution)/shard_map/reduce_scatter | solution.py:305
  1330.1 32.5 all-to-all-start.1
  1335.9 32.9 copy-start.121
  1335.9 34.7 copy-start.120
  1335.9 41.4 %copy-start.102 = (f32[2048]{0:T(1024)S(1)}, f32[2048]{0:T(1024)}, u32[]{:S(2)}) copy-start(f32[2048]{0:T(1024)} %get-tuple-element.558) | copy-start | bytes 24580
  1335.9 41.4 %copy-start.115 = (f32[1024]{0:T(1024)S(1)}, f32[1024]{0:T(1024)}, u32[]{:S(2)}) copy-start(f32[1024]{0:T(1024)} %get-tuple-element.633) | copy-start | bytes 12292
  1362.6 65.6 %all-to-all-start.3 = ((bf16[8,16,2048]{2,1,0:T(8,128)(2,1)}), bf16[8,16,2048]{2,1,0:T(8,128)(2,1)S(1)}, u32[]{:S(2)}, u32[]{:S(2)}) async-start(bf16[8,16,2048]{2,1,0:T(8,128)(2,1)} %bitcast.33), calls=%async_computation.3 | async-start | bytes 1048576 | tf_op jit(solution)/shard_map/all_to_all | solution.py:284
  1861.8 1604.7 %copy-start.1 = (bf16[128,2048]{1,0:T(8,128)(2,1)S(1)}, bf16[128,2048]{1,0:T(8,128)(2,1)}, u32[]{:S(2)}) copy-start(bf16[128,2048]{1,0:T(8,128)(2,1)} %param.22) | copy-start | bytes 1572868
  (149 other events, 826.2 us)
Sparse Core Ops, SparseCore 0:
  52.9 31.0 all-reduce.72
  538.9 37.6 all-reduce.74
  603.8 36.4 all-reduce.76
  1210.7 51.5 all-reduce.82
  1266.1 61.9 reduce-scatter.18
  1332.6 529.1 all-reduce.78
  1866.6 973.0 all-reduce.80
  2843.7 52.7 reduce-scatter.12
  2900.8 60.9 reduce-scatter.10
  2965.5 61.6 reduce-scatter.8
  3031.8 148.5 reduce-scatter.14
  3184.6 281.7 reduce-scatter.16
where the time goes:
time: 3520 us; the launch traced here: 3470 us
  waiting for transfers between devices  2120 us (60%)
  local copies, waits for them, and re-layouts  802 us (23%)
  other arithmetic  302 us (9%)
  matrix products  139 us (4%)
  blocking collectives  57.8 us (2%)
    unnamed x15, waiting for transfers between devices  1410 us
    pad x40, local copies, waits for them, and re-layouts, retreat(): lax.associative_scan(combine, (jnp.flip(following, 0), jnp.flip(emitted,...  286 us
    reduce_scatter x1, waiting for transfers between devices, body(): lax.psum_scatter(down_grad, 'dp', scatter_dimension=1, tiled=True)  286 us
    pad x40, local copies, waits for them, and re-layouts, advance(): lax.associative_scan(combine, (factor, source), axis=0)  277 us
    reduce_scatter x1, waiting for transfers between devices, body(): lax.psum_scatter(out_grad, 'dp', scatter_dimension=1, tiled=True)  153 us
  transfers between devices with their start and end apart: 16, of which 11 were waited for; matrix products, arithmetic and copies ran while one was open for 18% of the time, Pallas kernels for 0%

commit v1 on v0

v1 whole, which is shorter than its diff:
```python
import functools

import jax
import jax.numpy as jnp
from jax import lax
from jax.experimental import pallas as pl
from jax.experimental.pallas import tpu as pltpu
from jax.sharding import PartitionSpec as P

EPS = 1e-05
LOG2E = 1.4426950408889634
LANES = 128
ROWS = 16
GROUP = 8


def rms_scale(values):
    return lax.rsqrt(jnp.mean(values * values, axis=-1, keepdims=True) + EPS)


def rms_back(upstream, values, row_scale):
    return row_scale * (
        upstream
        - values * row_scale * row_scale * jnp.mean(upstream * values, axis=-1, keepdims=True)
    )


def silu_slope(values):
    logistic = jax.nn.sigmoid(values)
    return logistic * (1.0 + values * (1.0 - logistic))


def sequence_offsets(lengths_row, row_count):
    starts = jnp.cumsum(lengths_row) - lengths_row
    positions = jnp.arange(row_count, dtype=jnp.int32)
    begins = jnp.max(jnp.where(starts[None, :] <= positions[:, None], starts[None, :], 0), axis=1)
    return positions - begins


def shift_down(values, amount):
    if amount == 0:
        return values
    padding = jnp.zeros((amount,) + values.shape[1:], values.dtype)
    return jnp.concatenate([padding, values[:-amount]], axis=0)


def shift_up(values, amount):
    if amount == 0:
        return values
    padding = jnp.zeros((amount,) + values.shape[1:], values.dtype)
    return jnp.concatenate([values[amount:], padding], axis=0)


def causal_conv(inner_part, weight, conv_bias, offset):
    conv_taps = weight.shape[0]
    summed = conv_bias[None, :] + weight[conv_taps - 1][None, :] * inner_part
    for distance in range(1, conv_taps):
        valid_rows = (offset >= distance).astype(jnp.float32)[:, None]
        summed = (
            summed
            + weight[conv_taps - 1 - distance][None, :]
            * shift_down(inner_part, distance)
            * valid_rows
        )
    return summed


def scan_fwd_kernel(keep_ref, step_ref, u_ref, rate_ref, b_ref, c_ref, states_ref, y_ref, state_ref):
    width = step_ref.shape[1]
    spread = rate_ref.shape[0]
    block = pl.program_id(0)

    @pl.when(block == 0)
    def _():
        state_ref[...] = jnp.zeros_like(state_ref)

    tiles = width // LANES
    slices = [pl.ds(j * LANES, LANES) for j in range(tiles)]

    mine = lax.broadcasted_iota(jnp.int32, (GROUP, LANES), 0)

    def wide(ref, base, r, j):
        tile = ref[pl.ds(base, GROUP), slices[j]]
        return jnp.broadcast_to(tile[r : r + 1], (spread, LANES))

    def group(k, state):
        base = pl.multiple_of(k * GROUP, GROUP)
        state = list(state)
        y = [jnp.zeros((GROUP, LANES), jnp.float32)] * tiles
        for r in range(GROUP):
            keep = keep_ref[block * ROWS + base + r]
            b_row = b_ref[base + r]
            c_row = c_ref[base + r]
            for j in range(tiles):
                step = wide(step_ref, base, r, j)
                u = wide(u_ref, base, r, j)
                factor = jnp.exp2(step * rate_ref[:, slices[j]]) * keep
                state[j] = factor * state[j] + u * b_row
                states_ref[base + r, :, slices[j]] = state[j]
                y[j] = jnp.where(mine == r, jnp.sum(c_row * state[j], axis=0, keepdims=True), y[j])
        for j in range(tiles):
            y_ref[pl.ds(base, GROUP), slices[j]] = y[j]
        return tuple(state)

    state = tuple(state_ref[:, s] for s in slices)
    state = lax.fori_loop(0, ROWS // GROUP, group, state)
    for j in range(tiles):
        state_ref[:, slices[j]] = state[j]


def scan_fwd(keep, step_size, u, rate2, b_wide, c_wide):
    rows, width = step_size.shape
    n = rate2.shape[0]
    row_spec = pl.BlockSpec((ROWS, width), lambda i: (i, 0))
    wide_spec = pl.BlockSpec((ROWS, n, LANES), lambda i: (i, 0, 0))
    return pl.pallas_call(
        scan_fwd_kernel,
        grid=(rows // ROWS,),
        in_specs=[
            pl.BlockSpec(memory_space=pltpu.SMEM),
            row_spec,
            row_spec,
            pl.BlockSpec((n, width), lambda i: (0, 0)),
            wide_spec,
            wide_spec,
        ],
        out_specs=[pl.BlockSpec((ROWS, n, width), lambda i: (i, 0, 0)), row_spec],
        out_shape=[
            jax.ShapeDtypeStruct((rows, n, width), jnp.float32),
            jax.ShapeDtypeStruct((rows, width), jnp.float32),
        ],
        scratch_shapes=[pltpu.VMEM((n, width), jnp.float32)],
        name="scan_fwd",
    )(keep, step_size, u, rate2, b_wide, c_wide)


def scan_bwd_kernel(
    keep_ref,
    step_ref,
    conv_ref,
    ds_ref,
    rate_ref,
    b_ref,
    c_ref,
    states_ref,
    before_ref,
    d_step_ref,
    g_ref,
    db_ref,
    dc_ref,
    decay_ref,
    carry_ref,
):
    width = step_ref.shape[1]
    spread = rate_ref.shape[0]
    index = pl.program_id(0)
    block = pl.num_programs(0) - 1 - index

    @pl.when(index == 0)
    def _():
        carry_ref[...] = jnp.zeros_like(carry_ref)
        decay_ref[...] = jnp.zeros_like(decay_ref)

    tiles = width // LANES
    slices = [pl.ds(j * LANES, LANES) for j in range(tiles)]

    mine = lax.broadcasted_iota(jnp.int32, (GROUP, LANES), 0)

    def wide(ref, base, r, j):
        tile = ref[pl.ds(base, GROUP), slices[j]]
        return jnp.broadcast_to(tile[r : r + 1], (spread, LANES))

    def group(k, carry):
        base = pl.multiple_of(ROWS - GROUP - k * GROUP, GROUP)
        carry = list(carry)
        zero = jnp.zeros((GROUP, LANES), jnp.float32)
        d_step, weighted = [zero] * tiles, [zero] * tiles
        for r in reversed(range(GROUP)):
            t = base + r
            keep = keep_ref[block * ROWS + t]
            b_row = b_ref[t]
            c_row = c_ref[t]
            db = jnp.zeros((spread, LANES), jnp.float32)
            dc = jnp.zeros((spread, LANES), jnp.float32)
            for j in range(tiles):
                step = wide(step_ref, base, r, j)
                conv = wide(conv_ref, base, r, j)
                ds = wide(ds_ref, base, r, j)
                rate = rate_ref[:, slices[j]]
                factor = jnp.exp2(step * (rate * LOG2E)) * keep
                grad = c_row * ds + carry[j]
                passed = factor * grad
                if r == 0:
                    previous = jnp.where(
                        base == 0,
                        before_ref[0, :, slices[j]],
                        states_ref[jnp.maximum(t - 1, 0), :, slices[j]],
                    )
                else:
                    previous = states_ref[t - 1, :, slices[j]]
                via = passed * previous
                g = jnp.sum(grad * b_row, axis=0, keepdims=True)
                through = jnp.sum(via * rate, axis=0, keepdims=True) + conv[:1] * g
                d_step[j] = jnp.where(mine == r, through, d_step[j])
                weighted[j] = jnp.where(mine == r, g, weighted[j])
                decay_ref[:, slices[j]] += via * step
                db = db + grad * (step * conv)
                dc = dc + states_ref[t, :, slices[j]] * ds
                carry[j] = passed
            db_ref[t] = db
            dc_ref[t] = dc
        for j in range(tiles):
            d_step_ref[pl.ds(base, GROUP), slices[j]] = d_step[j]
            g_ref[pl.ds(base, GROUP), slices[j]] = weighted[j]
        return tuple(carry)

    carry = tuple(carry_ref[:, s] for s in slices)
    carry = lax.fori_loop(0, ROWS // GROUP, group, carry)
    for j in range(tiles):
        carry_ref[:, slices[j]] = carry[j]


def scan_bwd(keep, step_size, conv_in, d_scanned, rate, b_wide, c_wide, states):
    rows, width = step_size.shape
    n = rate.shape[0]
    last = rows // ROWS - 1
    row_spec = pl.BlockSpec((ROWS, width), lambda i: (last - i, 0))
    wide_spec = pl.BlockSpec((ROWS, n, LANES), lambda i: (last - i, 0, 0))
    return pl.pallas_call(
        scan_bwd_kernel,
        grid=(rows // ROWS,),
        in_specs=[
            pl.BlockSpec(memory_space=pltpu.SMEM),
            row_spec,
            row_spec,
            row_spec,
            pl.BlockSpec((n, width), lambda i: (0, 0)),
            wide_spec,
            wide_spec,
            pl.BlockSpec((ROWS, n, width), lambda i: (last - i, 0, 0)),
            pl.BlockSpec((1, n, width), lambda i: (jnp.maximum((last - i) * ROWS - 1, 0), 0, 0)),
        ],
        out_specs=[
            row_spec,
            row_spec,
            wide_spec,
            wide_spec,
            pl.BlockSpec((n, width), lambda i: (0, 0)),
        ],
        out_shape=[
            jax.ShapeDtypeStruct((rows, width), jnp.float32),
            jax.ShapeDtypeStruct((rows, width), jnp.float32),
            jax.ShapeDtypeStruct((rows, n, LANES), jnp.float32),
            jax.ShapeDtypeStruct((rows, n, LANES), jnp.float32),
            jax.ShapeDtypeStruct((n, width), jnp.float32),
        ],
        scratch_shapes=[pltpu.VMEM((n, width), jnp.float32)],
        name="scan_bwd",
    )(keep, step_size, conv_in, d_scanned, rate, b_wide, c_wide, states, states)


def one_hot_rows(places, count):
    return (jnp.arange(count, dtype=jnp.int32)[:, None] == places[None, :]).astype(jnp.bfloat16)


def rank_within(values):
    return jnp.sum((values[None, :] < values[:, None]).astype(jnp.int32), axis=1)


def slots_of(index, row_count, share):
    peer = index // row_count
    rows = jnp.arange(row_count, dtype=jnp.int32)
    earlier = (peer[None, :] == peer[:, None]) & (rows[None, :] < rows[:, None])
    return peer * share + jnp.sum(earlier.astype(jnp.int32), axis=1)


def pick_rows(selector, values):
    return jnp.dot(selector, values, preferred_element_type=jnp.float32).astype(jnp.bfloat16)


def body(
    tokens,
    cotangent,
    lengths,
    owner_index,
    arrival_index,
    norm_gain_mixer,
    in_weight,
    conv_weight,
    conv_bias,
    xproj_weight,
    dt_weight,
    dt_bias,
    a_log,
    skip_gain,
    out_weight,
    norm_gain_mlp,
    gate_up_weight,
    down_weight,
    *,
    n_dp,
):
    row_count, model_width = tokens.shape
    inner_width = in_weight.shape[2]
    hidden_width = gate_up_weight.shape[2]
    rank_width = dt_weight.shape[0]
    state_width = a_log.shape[0]
    share = row_count // n_dp
    me = lax.axis_index("dp")

    def exchange(values):
        return lax.all_to_all(values, "dp", split_axis=0, concat_axis=0, tiled=True)

    def columns_for_all(values):
        return lax.all_to_all(values, "dp", split_axis=1, concat_axis=0, tiled=True)

    def gather_rows(values):
        return lax.all_gather(values, "dp", axis=0, tiled=True)

    send_select = one_hot_rows(rank_within(owner_index), row_count)
    owner_slots = slots_of(arrival_index, row_count, share)
    take_select = jnp.transpose(one_hot_rows(owner_slots, row_count))
    owned_bf16 = pick_rows(take_select, exchange(pick_rows(send_select, tokens)))
    owned_grad = pick_rows(take_select, exchange(pick_rows(send_select, cotangent)))
    grad_all = gather_rows(owned_grad)
    owned_rows = owned_bf16.astype(jnp.float32)
    offset = sequence_offsets(lengths[0], row_count)
    keep_mask = (offset > 0).astype(jnp.float32)
    scale_mixer = rms_scale(owned_rows)
    normed = (owned_rows * scale_mixer * norm_gain_mixer).astype(jnp.bfloat16)
    normed_cols = columns_for_all(normed)
    in_flat = in_weight.reshape(model_width, 2 * inner_width)
    projected = jnp.dot(normed, in_flat, preferred_element_type=jnp.float32)
    inner_part = projected[:, :inner_width]
    gate_z = projected[:, inner_width:]
    conv_pre = causal_conv(inner_part, conv_weight, conv_bias, offset)
    conv_out = jax.nn.silu(conv_pre).astype(jnp.bfloat16)
    conv_in = conv_out.astype(jnp.float32)
    pieces = lax.psum(jnp.dot(conv_out, xproj_weight, preferred_element_type=jnp.float32), "tensor")
    dt_low = pieces[:, :rank_width].astype(jnp.bfloat16)
    b_proj = pieces[:, rank_width : rank_width + state_width]
    c_proj = pieces[:, rank_width + state_width :]
    b_wide = jnp.broadcast_to(b_proj[:, :, None], (row_count, state_width, LANES))
    c_wide = jnp.broadcast_to(c_proj[:, :, None], (row_count, state_width, LANES))
    dt_pre = jnp.dot(dt_low, dt_weight, preferred_element_type=jnp.float32) + dt_bias
    step_size = jax.nn.softplus(dt_pre)
    decay_rate = -jnp.exp(a_log)
    states, scan_part = scan_fwd(
        keep_mask, step_size, step_size * conv_in, decay_rate * LOG2E, b_wide, c_wide
    )
    scanned = scan_part + skip_gain * conv_in
    silu_z = jax.nn.silu(gate_z)
    gated = (scanned * silu_z).astype(jnp.bfloat16)
    gated_all = gather_rows(gated)
    mixer_out = lax.psum(jnp.dot(gated, out_weight, preferred_element_type=jnp.float32), "tensor")
    hidden_in = owned_rows + mixer_out
    scale_mlp = rms_scale(hidden_in)
    normed_mlp = (hidden_in * scale_mlp * norm_gain_mlp).astype(jnp.bfloat16)
    gate_flat = gate_up_weight.reshape(model_width, 2 * hidden_width)

    def mlp_parts(rows, grads):
        gate_up = jnp.dot(rows, gate_flat, preferred_element_type=jnp.float32)
        gate_part = gate_up[:, :hidden_width]
        up_part = gate_up[:, hidden_width:]
        hidden = (jax.nn.silu(gate_part) * up_part).astype(jnp.bfloat16)
        d_hidden = jnp.einsum("td,fd->tf", grads, down_weight, preferred_element_type=jnp.float32)
        d_gate = d_hidden * up_part * silu_slope(gate_part)
        d_up = d_hidden * jax.nn.silu(gate_part)
        return hidden, d_gate.astype(jnp.bfloat16), d_up.astype(jnp.bfloat16)

    hidden, d_gate, d_up = mlp_parts(normed_mlp, owned_grad)
    d_gate_up = jnp.concatenate([d_gate, d_up], axis=1)
    d_normed_mlp = lax.psum(
        jnp.einsum("tk,dk->td", d_gate_up, gate_flat, preferred_element_type=jnp.float32), "tensor"
    )
    normed_mlp_all = gather_rows(normed_mlp)
    down_out = lax.psum(jnp.dot(hidden, down_weight, preferred_element_type=jnp.float32), "tensor")
    output_own = (hidden_in + down_out).astype(jnp.bfloat16)
    upstream = owned_grad.astype(jnp.float32)
    gain_mlp_grad = jnp.sum(d_normed_mlp * hidden_in * scale_mlp, axis=0)
    d_hidden_in = upstream + rms_back(d_normed_mlp * norm_gain_mlp, hidden_in, scale_mlp)
    d_mixed = d_hidden_in.astype(jnp.bfloat16)
    d_mixed_cols = columns_for_all(d_mixed)
    d_gated = jnp.einsum("td,cd->tc", d_mixed, out_weight, preferred_element_type=jnp.float32)
    d_scanned = d_gated * silu_z
    d_gate_z = d_gated * scanned * silu_slope(gate_z)
    skip_grad = jnp.sum(d_scanned * conv_in, axis=0)
    d_step, b_weighted, db_part, dc_part, decay_grad = scan_bwd(
        keep_mask, step_size, conv_in, d_scanned, decay_rate, b_wide, c_wide, states
    )
    a_log_grad = decay_grad * decay_rate
    d_dt_pre = d_step * jax.nn.sigmoid(dt_pre)
    dt_bias_grad = jnp.sum(d_dt_pre, axis=0)
    d_dt_rounded = d_dt_pre.astype(jnp.bfloat16)
    dt_weight_grad = jnp.einsum(
        "tr,tc->rc", dt_low, d_dt_rounded, preferred_element_type=jnp.float32
    )
    d_dt_low = jnp.einsum("tc,rc->tr", d_dt_rounded, dt_weight, preferred_element_type=jnp.float32)
    d_pieces = lax.psum(
        jnp.concatenate([d_dt_low, jnp.sum(db_part, axis=2), jnp.sum(dc_part, axis=2)], axis=1),
        "tensor",
    ).astype(jnp.bfloat16)
    xproj_grad = jnp.einsum("tc,tk->ck", conv_out, d_pieces, preferred_element_type=jnp.float32)
    d_conv = (
        d_scanned * skip_gain
        + step_size * b_weighted
        + jnp.einsum("tk,ck->tc", d_pieces, xproj_weight, preferred_element_type=jnp.float32)
    )
    d_conv_pre = d_conv * silu_slope(conv_pre)
    conv_bias_grad = jnp.sum(d_conv_pre, axis=0)
    conv_taps = conv_weight.shape[0]
    tap_grads = []
    d_inner = jnp.zeros_like(inner_part)
    for distance in range(conv_taps):
        valid_grad = d_conv_pre * (offset >= distance).astype(jnp.float32)[:, None]
        tap_grads.append(jnp.sum(valid_grad * shift_down(inner_part, distance), axis=0))
        d_inner = d_inner + conv_weight[conv_taps - 1 - distance][None, :] * shift_up(
            valid_grad, distance
        )
    conv_weight_grad = jnp.stack(tap_grads[::-1], axis=0)
    d_projected = jnp.concatenate([d_inner, d_gate_z], axis=1).astype(jnp.bfloat16)
    d_projected_all = gather_rows(d_projected)
    d_normed = lax.psum(
        jnp.einsum("tk,dk->td", d_projected, in_flat, preferred_element_type=jnp.float32), "tensor"
    )
    gain_mixer_grad = jnp.sum(d_normed * owned_rows * scale_mixer, axis=0)
    d_tokens = d_hidden_in + rms_back(d_normed * norm_gain_mixer, owned_rows, scale_mixer)

    back_select = one_hot_rows(rank_within(arrival_index), row_count)
    arrive_select = jnp.transpose(one_hot_rows(slots_of(owner_index, row_count, share), row_count))
    output = pick_rows(arrive_select, exchange(pick_rows(back_select, output_own)))
    tokens_grad = pick_rows(
        arrive_select, exchange(pick_rows(back_select, d_tokens.astype(jnp.bfloat16)))
    )

    share_width = model_width // n_dp

    def my_columns(values):
        return lax.dynamic_slice_in_dim(values, me * share_width, share_width, axis=1)

    hidden_all, d_gate_all, d_up_all = mlp_parts(normed_mlp_all, grad_all)
    grad_cols = my_columns(grad_all)
    down_grad = jnp.einsum("tf,td->fd", hidden_all, grad_cols, preferred_element_type=jnp.float32)
    mlp_cols = my_columns(normed_mlp_all)

    def weight_grad(rows, upstream_rows):
        return jnp.einsum("td,tk->dk", rows, upstream_rows, preferred_element_type=jnp.float32)

    gate_up_grad = jnp.stack(
        [weight_grad(mlp_cols, d_gate_all), weight_grad(mlp_cols, d_up_all)], axis=1
    )
    out_grad = jnp.einsum("tc,td->cd", gated_all, d_mixed_cols, preferred_element_type=jnp.float32)
    in_grad = weight_grad(normed_cols, d_projected_all).reshape(share_width, 2, inner_width)

    def for_peers(values, axis):
        if values.ndim == 1:
            return values.reshape(n_dp, 1, -1)
        if axis == 0:
            return values.reshape(n_dp, values.shape[0] // n_dp, values.shape[1])
        return values.reshape(values.shape[0], n_dp, -1).transpose(1, 0, 2)

    small = [
        (gain_mixer_grad, 0),
        (conv_weight_grad, 1),
        (conv_bias_grad, 0),
        (xproj_grad, 0),
        (dt_weight_grad, 0),
        (dt_bias_grad, 0),
        (a_log_grad, 1),
        (skip_grad, 0),
        (gain_mlp_grad, 0),
    ]
    blocks = [for_peers(values, axis) for values, axis in small]
    packed = jnp.concatenate([block.reshape(n_dp, -1) for block in blocks], axis=1)
    summed = jnp.sum(exchange(packed), axis=0)
    results = []
    start = 0
    for (values, _), block in zip(small, blocks):
        size = block.shape[1] * block.shape[2]
        piece = summed[start : start + size]
        results.append(piece if values.ndim == 1 else piece.reshape(block.shape[1:]))
        start += size
    return (
        output,
        tokens_grad,
        results[0],
        in_grad,
        results[1],
        results[2],
        results[3],
        results[4],
        results[5],
        results[6],
        results[7],
        out_grad,
        results[8],
        gate_up_grad,
        down_grad,
    )


def solution(mesh):
    in_specs = (
        P("dp", None),
        P("dp", None),
        P("dp", None),
        P("dp"),
        P("dp"),
        P(),
        P(None, None, "tensor"),
        P(None, "tensor"),
        P("tensor"),
        P("tensor", None),
        P(None, "tensor"),
        P("tensor"),
        P(None, "tensor"),
        P("tensor"),
        P("tensor", None),
        P(),
        P(None, None, "tensor"),
        P("tensor", None),
    )
    out_specs = (
        P("dp", None),
        P("dp", None),
        P("dp"),
        P("dp", None, "tensor"),
        P(None, ("tensor", "dp")),
        P(("tensor", "dp")),
        P(("tensor", "dp"), None),
        P("dp", "tensor"),
        P(("tensor", "dp")),
        P(None, ("tensor", "dp")),
        P(("tensor", "dp")),
        P("tensor", "dp"),
        P("dp"),
        P("dp", None, "tensor"),
        P("tensor", "dp"),
    )
    step = functools.partial(body, n_dp=mesh.shape["dp"])
    return jax.shard_map(step, mesh=mesh, in_specs=in_specs, out_specs=out_specs, check_vma=False)
```

time: 3520 us -> 653 us (0.19); the launches traced: 3470 us -> 644 us
  waiting for transfers between devices: 2120 us -> 312 us
  local copies, waits for them, and re-layouts: 802 us -> 75.4 us
  other arithmetic: 302 us -> 26.6 us
  blocking collectives: 57.8 us -> 11.5 us
    unnamed x15 -> x8, waiting for transfers between devices: 1410 us -> 1.15 us
    reduce_scatter x5 -> x0, waiting for transfers between devices: 621 us -> none  [the longest x1 286 us: body(): lax.psum_scatter(down_grad, 'dp', scatter_dimension=1, tiled=True)]
    pad x80 -> x0, local copies, waits for them, and re-layouts: 563 us -> none  [the longest x40 286 us: retreat(): lax.associative_scan(combine, (jnp.flip(following, 0), jnp.flip(emitted,...]
    add x68 -> x2, other arithmetic: 139 us -> 0.02 us  [slots_of(): return peer * share + jnp.sum(earlier.astype(jnp.int32), axis=1)]
    all_gather x0 -> x4, waiting for transfers between devices: none -> 117 us  [gather_rows(): return lax.all_gather(values, 'dp', axis=0, tiled=True)]
    reshape x6 -> x2, local copies, waits for them, and re-layouts: 70 us -> 0.74 us  [body(): piece.reshape(block.shape[1:])]
    all_to_all x4 -> x7, waiting for transfers between devices: 23.3 us -> 76.7 us  [the longest x5 76.7 us: exchange(): return lax.all_to_all(values, 'dp', split_axis=0, concat_axis=0, tiled=True)]
    unnamed x1 -> x0, blocking collectives: 46.1 us -> none
  transfers between devices with their start and end apart: 16 -> 15, of which waited for: 11 -> 11; matrix products, arithmetic and copies ran while one was open for 18% -> 27% of each run, Pallas kernels for 0% -> 1%
where the time goes in v1:
time: 653 us; the launch traced here: 644 us
  waiting for transfers between devices  312 us (48%)
  matrix products  146 us (22%)
  local copies, waits for them, and re-layouts  75.4 us (12%)
  starting transfers between devices  36 us (6%)
  other arithmetic  26.6 us (4%)
  Pallas kernels  20.9 us (3%)
  between operations  15.2 us (2%)
  blocking collectives  11.5 us (2%)
    all_gather x4, waiting for transfers between devices, gather_rows(): return lax.all_gather(values, 'dp', axis=0, tiled=True)  117 us
    all_to_all x5, waiting for transfers between devices, exchange(): return lax.all_to_all(values, 'dp', split_axis=0, concat_axis=0, tiled=True)  76.7 us
    unnamed x127, local copies, waits for them, and re-layouts  51.5 us
    psum x1, waiting for transfers between devices, body(): lax.psum(jnp.dot(hidden, down_weight, preferred_element_type=jnp.float32)...  37.5 us
    psum x1, waiting for transfers between devices, body(): lax.psum(jnp.dot(conv_out, xproj_weight, preferred_element_type=jnp.float...  30.5 us
    psum x1, waiting for transfers between devices, body(): lax.psum(jnp.einsum('tk,dk->td', d_gate_up, gate_flat, preferred_element_...  29.8 us
    dot_general x2, matrix products, mlp_parts(): gate_up = jnp.dot(rows, gate_flat, preferred_element_type=jnp.float32)  29.8 us
    all_to_all x5, starting transfers between devices, exchange(): return lax.all_to_all(values, 'dp', split_axis=0, concat_axis=0, tiled=True)  26 us
  transfers between devices with their start and end apart: 15, of which 11 were waited for; matrix products, arithmetic and copies ran while one was open for 27% of the time, Pallas kernels for 1%

profile of v1, /device:TPU:0, one launch (start us, length us, event | category | flops | bytes accessed | tf_op | source)
XLA Modules:
  0.0 643.6 jit_solution(9457470477202243140)
XLA Ops:
  9.3 7.3 %all-to-all-start = ((bf16[8,16,2048]{2,1,0:T(8,128)(2,1)}), bf16[8,16,2048]{2,1,0:T(8,128)(2,1)S(1)}, u32[]{:S(2)}, u32[]{:S(2)}) async-start(bf16[8,16,2048]{2,1,0:T(8,128)(2,1)} %bitcast), calls=%async_computation | async-start | bytes 1048576 | tf_op jit(solution)/shard_map/all_to_all | solution.py:312
  19.1 10.2 %copy.79 = bf16[256,8,2,1024]{3,1,2,0:T(8,128)(2,1)} copy(bf16[256,8,2,1024]{3,2,1,0:T(2,128)(2,1)} %bitcast.112) | data formatting | bytes 16777216
  31.1 5.9 all-to-all-start.2
  37.7 4.9 fusion.60
  46.6 30.5 %all-reduce.12.cloned.1.call-done = f32[128,160]{0,1:T(8,128)} async-done(((f32[128,160]{0,1:T(8,128)}), f32[128,160]{0,1:T(8,128)}) %all-reduce.12.cloned.1.call-update) | async-done | bytes 81936 | tf_op jit(solution)/shard_map/psum | solution.py:339
  77.1 2.5 convert_multiply_fusion
  83.1 8.9 %scan_fwd.1 = (f32[128,16,1024]{2,1,0:T(8,128)}, f32[128,1024]{1,0:T(8,128)}) custom-call(f32[128]{0:T(128)} %get-tuple-element.139.keep_ref, f32[128,1024]{1,0:T(8,128)} %get-tuple-element.121.step_ref, f32[128,1024]{1,0:T(8,128)} %get-tuple-element.120.u_ref, f32[16,1024]{1,0:T(8,128)} %get-tuple-element.130.rate_ref, ...), custom_call_target="tpu_custom_call" | custom-call | tf_op jit(solution)/shard_map/scan_fwd/pallas_call | solution.py:116
  93.2 4.0 fusion.62
  97.4 17.3 %copy.80 = bf16[256,8,2,2048]{3,1,2,0:T(8,128)(2,1)} copy(bf16[256,8,2,2048]{3,2,1,0:T(2,128)(2,1)} %bitcast.111) | data formatting | bytes 33554432
  115.9 19.1 %all-reduce.14.cloned.1.call-done = f32[128,2048]{1,0:T(8,128)} async-done(((f32[128,2048]{1,0:T(8,128)}), f32[128,2048]{1,0:T(8,128)}) %all-reduce.14.cloned.1.call-update) | async-done | bytes 1048592 | tf_op jit(solution)/shard_map/psum | solution.py:355
  137.3 8.3 %fusion.63 = f32[128,4096]{1,0:T(8,128)S(1)} fusion(bf16[128,2048]{1,0:T(8,128)(2,1)} %multiply_convert_fusion.13, bf16[2048,4096]{1,0:T(8,128)(2,1)} %bitcast.106), kind=kOutput, calls=%fused_computation.160 | convolution fusion | flops 2147483648 | bytes 19398656 | tf_op jit(solution)/shard_map/dot_general | solution.py:362
  145.7 8.1 %multiply_convert_fusion.11 = (bf16[128,2048]{1,0:T(8,128)(2,1)}, bf16[128,2048]{1,0:T(8,128)(2,1)}) fusion(f32[128,4096]{1,0:T(8,128)S(1)} %fusion.63, bf16[128,2048]{1,0:T(8,128)(2,1)S(1)} %copy-done.3, bf16[2048,2048]{1,0:T(8,128)(2,1)} %param.35), kind=kOutput, calls=%fused_computation.35 | convolution fusion | flops 1077149696 | bytes 12058624 | tf_op jit(solution)/shard_map/td,fd->tf/dot_general | solution.py:366
  153.8 12.7 %fusion.8 = f32[128,2048]{1,0:T(8,128)} fusion(bf16[2048,4096]{1,0:T(8,128)(2,1)} %bitcast.107, bf16[128,2048]{1,0:T(8,128)(2,1)} %get-tuple-element.113, bf16[128,2048]{1,0:T(8,128)(2,1)} %get-tuple-element.112), kind=kOutput, calls=%fused_computation.24 | convolution fusion | flops 2149580800 | bytes 18874368 | tf_op jit(solution)/shard_map/tk,dk->td/dot_general | solution.py:374
  167.0 6.3 fusion.15
  173.4 29.8 %all-reduce.16.cloned.1.call-done = f32[128,2048]{1,0:T(8,128)} async-done(((f32[128,2048]{1,0:T(8,128)}), f32[128,2048]{1,0:T(8,128)}) %all-reduce.16.cloned.1.call-update) | async-done | bytes 1048592 | tf_op jit(solution)/shard_map/psum | solution.py:373
  203.2 2.3 multiply_reduce_fusion
  207.2 3.2 multiply_reduce_fusion.6
  210.4 12.0 %scan_bwd.1 = (f32[128,1024]{1,0:T(8,128)}, f32[128,1024]{1,0:T(8,128)}, f32[128,16,128]{2,1,0:T(8,128)}, f32[128,16,128]{2,1,0:T(8,128)}, f32[16,1024]{1,0:T(8,128)}) custom-call(f32[128]{0:T(128)} %get-tuple-element.139.keep_ref, f32[128,1024]{1,0:T(8,128)} %get-tuple-element.121.step_ref, f32[128,1024]{1,0:T(8,128)} %get-tuple-element.107.conv_ref, ...), custom_call_target="tpu_custom_call" | custom-call | tf_op jit(solution)/shard_map/scan_bwd/pallas_call | solution.py:229
  231.4 11.5 %psum.46 = bf16[128,160]{0,1:T(8,128)(2,1)S(1)} all-reduce(f32[128,160]{0,1:T(8,128)S(1)} %pad_maximum_fusion.2), channel_id=1, replica_groups=mesh['dp'=8,'tensor'=4] {'tensor'}, use_global_device_ids=true, to_apply=%region_15.16 | all-reduce | flops 20480 | bytes 122880 | tf_op jit(solution)/shard_map/psum | solution.py:399
  243.0 3.6 multiply_reduce_fusion.8
  248.4 7.3 %fusion.50 = f32[128,2048]{1,0:T(8,128)} fusion(bf16[2048,2048]{1,0:T(8,128)(2,1)} %bitcast.110, bf16[128,1024]{1,0:T(8,128)(2,1)S(1)} %copy-done.18, bf16[128,1024]{1,0:T(8,128)(2,1)S(1)} %get-tuple-element.115), kind=kOutput, calls=%fused_computation.148 | convolution fusion | flops 1074790400 | bytes 9961472 | tf_op jit(solution)/shard_map/tk,dk->td/dot_general | solution.py:424
  264.4 5.5 all-to-all-start.6
  270.0 37.5 %all-reduce.18.cloned.1.call-done = (f32[128,2048]{1,0:T(8,128)}, f32[128,2048]{1,0:T(8,128)}) async-done(((f32[128,2048]{1,0:T(8,128)}, f32[128,2048]{1,0:T(8,128)}), (f32[128,2048]{1,0:T(8,128)}, f32[128,2048]{1,0:T(8,128)})) %all-reduce.18.cloned.1.call-update) | async-done | bytes 2097168 | tf_op jit(solution)/shard_map/psum | solution.py:377
  312.8 2.3 convolution_convert_fusion.5
  315.1 5.5 all-to-all-start.1
  322.5 3.0 convolution_convert_fusion.1
  325.5 15.8 %all-to-all-done.1 = bf16[8,16,2048]{2,1,0:T(8,128)(2,1)} async-done(((bf16[8,16,2048]{2,1,0:T(8,128)(2,1)}), bf16[8,16,2048]{2,1,0:T(8,128)(2,1)}, u32[]{:S(2)}, u32[]{:S(2)}) %all-to-all-start.1) | async-done | bytes 524320 | tf_op jit(solution)/shard_map/all_to_all | solution.py:312
  341.3 3.7 all-to-all-start.3
  347.4 3.7 copy.66
  351.1 22.1 %all-to-all-done.3 = bf16[8,16,2048]{2,1,0:T(8,128)(2,1)S(1)} async-done(((bf16[8,16,2048]{2,1,0:T(8,128)(2,1)}), bf16[8,16,2048]{2,1,0:T(8,128)(2,1)S(1)}, u32[]{:S(2)}, u32[]{:S(2)}) %all-to-all-start.3) | async-done | bytes 524320 | tf_op jit(solution)/shard_map/all_to_all | solution.py:312
  373.2 3.6 all-to-all-start.4
  378.8 2.2 convolution_convert_fusion.4
  382.1 3.6 fusion.65
  385.7 38.7 %all-to-all-done.4 = f32[8,1,40320]{2,1,0:T(1,128)S(1)} async-done(((f32[8,1,40320]{2,1,0:T(1,128)}), f32[8,1,40320]{2,1,0:T(1,128)S(1)}, u32[]{:S(2)}, u32[]{:S(2)}) %all-to-all-start.4) | async-done | bytes 1290272 | tf_op jit(solution)/shard_map/all_to_all | solution.py:312
  424.4 3.6 all-to-all-start.5
  432.8 42.5 %all-gather.11.cloned.1.call-done = bf16[1024,2048]{1,0:T(8,128)(2,1)} async-done(((bf16[128,2048]{1,0:T(8,128)(2,1)}), bf16[1024,2048]{1,0:T(8,128)(2,1)}) %all-gather.11.cloned.1.call-update) | async-done | bytes 4194320 | tf_op jit(solution)/shard_map/all_gather | solution.py:318
  475.3 14.5 %fusion.66 = f32[1024,2048]{1,0:T(8,128)} fusion(bf16[1024,2048]{1,0:T(8,128)(2,1)} %all-gather.11.cloned.1.call-done, bf16[2048,2048]{1,0:T(8,128)(2,1)} %param.35), kind=kOutput, calls=%fused_computation.163 | convolution fusion | flops 8589934592 | bytes 20971520 | tf_op jit(solution)/shard_map/td,fd->tf/dot_general | solution.py:366
  489.8 60.0 %all-gather.9.cloned.1.call-done = bf16[1024,2048]{1,0:T(8,128)(2,1)} async-done(((bf16[128,2048]{1,0:T(8,128)(2,1)}), bf16[1024,2048]{1,0:T(8,128)(2,1)}) %all-gather.9.cloned.1.call-update) | async-done | bytes 4194320 | tf_op jit(solution)/shard_map/all_gather | solution.py:318
  549.8 21.5 %fusion.67 = f32[1024,4096]{1,0:T(8,128)S(1)} fusion(bf16[1024,2048]{1,0:T(8,128)(2,1)} %all-gather.9.cloned.1.call-done, bf16[2048,4096]{1,0:T(8,128)(2,1)} %bitcast.108), kind=kOutput, calls=%fused_computation.164 | convolution fusion | flops 17179869184 | bytes 37748736 | tf_op jit(solution)/shard_map/dot_general | solution.py:362
  571.3 5.7 copy-done.56
  577.1 5.3 fusion.5
  582.3 11.1 %fusion.4 = f32[256,1,2048]{2,0,1:T(8,128)S(1)} fusion(f32[1024,2048]{1,0:T(8,128)} %fusion.66, f32[1024,4096]{1,0:T(8,128)} %copy-done.56, bf16[1024,2048]{1,0:T(8,128)(2,1)} %all-gather.9.cloned.1.call-done, s32[]{:T(128)S(6)} %select_n.24), kind=kOutput, calls=%fused_computation.9 | convolution fusion | flops 1094713344 | bytes 27787268 | tf_op jit(solution)/shard_map/td,tk->dk/dot_general | solution.py:447
  594.0 5.3 copy.73
  599.2 9.7 %fusion.2 = f32[2048,256]{1,0:T(8,128)} fusion(f32[1024,4096]{1,0:T(8,128)} %copy-done.56, bf16[1024,2048]{1,0:T(8,128)(2,1)} %all-gather.11.cloned.1.call-done, s32[]{:T(128)S(6)} %select_n.24), kind=kOutput, calls=%fused_computation.6 | convolution fusion | flops 1086324736 | bytes 19398660 | tf_op jit(solution)/shard_map/tf,td->fd/dot_general | solution.py:443
  609.0 14.7 %all-gather.5.cloned.1.call-done = bf16[1024,2048]{1,0:T(8,128)(2,1)} async-done(((bf16[128,2048]{1,0:T(8,128)(2,1)}), bf16[1024,2048]{1,0:T(8,128)(2,1)}) %all-gather.5.cloned.1.call-update) | async-done | bytes 4194320 | tf_op jit(solution)/shard_map/all_gather | solution.py:318
  623.6 6.4 copy.76
  630.0 3.5 fusion.64
  633.6 2.9 copy.71
  (215 shorter events, 58.8 us)
Async XLA Ops:
  9.3 21.8 %all-to-all-start = ((bf16[8,16,2048]{2,1,0:T(8,128)(2,1)}), bf16[8,16,2048]{2,1,0:T(8,128)(2,1)S(1)}, u32[]{:S(2)}, u32[]{:S(2)}) async-start(bf16[8,16,2048]{2,1,0:T(8,128)(2,1)} %bitcast), calls=%async_computation | async-start | bytes 1048576 | tf_op jit(solution)/shard_map/all_to_all | solution.py:312
  19.0 10.3 %copy-start.53 = (s32[128]{0:T(128)S(1)}, s32[128]{0:T(128)}, u32[]{:S(2)}) copy-start(s32[128]{0:T(128)} %param.22) | copy-start | bytes 1540
  19.0 10.8 %copy-start.34 = (f32[4,1024]{1,0:T(4,128)S(1)}, f32[4,1024]{1,0:T(4,128)}, u32[]{:S(2)}) copy-start(f32[4,1024]{1,0:T(4,128)} %param.25) | copy-start | bytes 49156
  19.1 10.8 %copy-start.21 = (bf16[128,2048]{1,0:T(8,128)(2,1)S(1)}, bf16[128,2048]{1,0:T(8,128)(2,1)}, u32[]{:S(2)}) copy-start(bf16[128,2048]{1,0:T(8,128)(2,1)} %param.19) | copy-start | bytes 1572868
  19.1 18.4 %copy-start.25 = (f32[2048]{0:T(1024)S(1)}, f32[2048]{0:T(1024)}, u32[]{:S(2)}) copy-start(f32[2048]{0:T(1024)} %param.23) | copy-start | bytes 24580
  29.9 12.9 %copy-start.43 = (f32[128]{0:T(128)}, f32[128]{0:T(128)S(1)}, u32[]{:S(2)}) copy-start(f32[128]{0:T(128)S(1)} %get-tuple-element.136) | copy-start | bytes 1540
  29.9 12.9 %copy-start.44 = (f32[128]{0:T(128)}, f32[128]{0:T(128)S(1)}, u32[]{:S(2)}) copy-start(f32[128]{0:T(128)S(1)} %get-tuple-element.137) | copy-start | bytes 1540
  29.9 13.0 %copy-start.45 = (f32[128]{0:T(128)}, f32[128]{0:T(128)S(1)}, u32[]{:S(2)}) copy-start(f32[128]{0:T(128)S(1)} %get-tuple-element.138) | copy-start | bytes 1540
  29.9 12.9 %copy-start.26 = (f32[1,1024]{1,0:T(1,128)}, f32[1,1024]{1,0:T(1,128)S(1)}, u32[]{:S(2)}) copy-start(f32[1,1024]{1,0:T(1,128)S(1)} %get-tuple-element.133) | copy-start | bytes 12292
  29.9 12.9 %copy-start.28 = (f32[1,1024]{1,0:T(1,128)}, f32[1,1024]{1,0:T(1,128)S(1)}, u32[]{:S(2)}) copy-start(f32[1,1024]{1,0:T(1,128)S(1)} %get-tuple-element.134) | copy-start | bytes 12292
  31.1 83.6 %all-to-all-start.2 = ((bf16[8,16,2048]{2,1,0:T(8,128)(2,1)}), bf16[8,16,2048]{2,1,0:T(8,128)(2,1)S(1)}, u32[]{:S(2)}, u32[]{:S(2)}) async-start(bf16[8,16,2048]{2,1,0:T(8,128)(2,1)} %bitcast.9), calls=%async_computation.2 | async-start | bytes 1048576 | tf_op jit(solution)/shard_map/all_to_all | solution.py:312
  37.0 40.1 %all-reduce.12.cloned.1.call-start = ((), (), s32[]{:S(2)}) async-start(), calls=%async_computation.7 | async-start | bytes 163840 | tf_op jit(solution)/shard_map/psum | solution.py:339
  42.6 34.5 %copy-start.17 = (bf16[128,1024]{1,0:T(8,128)(2,1)S(1)}, bf16[128,1024]{1,0:T(8,128)(2,1)}, u32[]{:S(2)}) copy-start(bf16[128,1024]{1,0:T(8,128)(2,1)} %param.28) | copy-start | bytes 786436
  42.6 34.5 %copy-start.47 = (f32[1024]{0:T(1024)S(1)}, f32[1024]{0:T(1024)}, u32[]{:S(2)}) copy-start(f32[1024]{0:T(1024)} %param.29) | copy-start | bytes 12292
  45.8 46.1 %copy-start.35 = (f32[1024]{0:T(1024)S(1)}, f32[1024]{0:T(1024)}, u32[]{:S(2)}) copy-start(f32[1024]{0:T(1024)} %param.31) | copy-start | bytes 12292
  45.8 89.1 %all-reduce.14.cloned.1.call-start = ((), (), s32[]{:S(2)}) async-start(), calls=%async_computation.8 | async-start | bytes 2097152 | tf_op jit(solution)/shard_map/psum | solution.py:355
  93.2 21.5 %copy-start.13 = (bf16[128,1024]{1,0:T(8,128)(2,1)}, bf16[128,1024]{1,0:T(8,128)(2,1)S(1)}, u32[]{:S(2)}) copy-start(bf16[128,1024]{1,0:T(8,128)(2,1)S(1)} %multiply_convert_fusion.17) | copy-start | bytes 786436
  97.2 106.0 %all-reduce.16.cloned.1.call-start = ((), (), s32[]{:S(2)}) async-start(), calls=%async_computation.9 | async-start | bytes 2097152 | tf_op jit(solution)/shard_map/psum | solution.py:373
  114.7 21.7 %copy-start.24 = (f32[2048]{0:T(1024)S(1)}, f32[2048]{0:T(1024)}, u32[]{:S(2)}) copy-start(f32[2048]{0:T(1024)} %param.33) | copy-start | bytes 24580
  136.4 69.1 %copy-start.39 = (f32[128]{0:T(128)}, f32[128]{0:T(128)S(1)}, u32[]{:S(2)}) copy-start(f32[128]{0:T(128)S(1)} %add_rsqrt_fusion) | copy-start | bytes 1540
  137.3 8.3 %copy-start.3 = (bf16[128,2048]{1,0:T(8,128)(2,1)S(1)}, bf16[128,2048]{1,0:T(8,128)(2,1)}, u32[]{:S(2)}) copy-start(bf16[128,2048]{1,0:T(8,128)(2,1)} %convolution_convert_fusion.2) | copy-start | bytes 1572868
  166.6 140.9 %all-reduce.18.cloned.1.call-start = ((), (), s32[]{:S(2)}) async-start(), calls=%async_computation.14 | async-start | bytes 4194304 | tf_op jit(solution)/shard_map/psum | solution.py:377
  248.4 8.5 %copy-start.54 = (s32[128]{0:T(128)S(1)}, s32[128]{0:T(128)}, u32[]{:S(2)}) copy-start(s32[128]{0:T(128)} %param.22) | copy-start | bytes 1540
  255.7 126.4 %all-gather.7.cloned.1.call-start = ((), (), s32[]{:S(2)}) async-start(), calls=%async_computation.11 | async-start | bytes 2359296 | tf_op jit(solution)/shard_map/all_gather | solution.py:318
  256.3 219.0 %all-gather.11.cloned.1.call-start = ((), (), s32[]{:S(2)}) async-start(), calls=%async_computation.13 | async-start | bytes 4718592 | tf_op jit(solution)/shard_map/all_gather | solution.py:318
  256.9 292.9 %all-gather.9.cloned.1.call-start = ((), (), s32[]{:S(2)}) async-start(), calls=%async_computation.12 | async-start | bytes 4718592 | tf_op jit(solution)/shard_map/all_gather | solution.py:318
  258.0 51.6 %copy-start.33 = (f32[1024]{0:T(1024)S(1)}, f32[1024]{0:T(1024)}, u32[]{:S(2)}) copy-start(f32[1024]{0:T(1024)} %get-tuple-element.94) | copy-start | bytes 12292
  258.0 51.6 %copy-start.36 = (f32[1024]{0:T(1024)S(1)}, f32[1024]{0:T(1024)}, u32[]{:S(2)}) copy-start(f32[1024]{0:T(1024)} %get-tuple-element.105) | copy-start | bytes 12292
  258.0 51.6 %copy-start.37 = (f32[1024]{0:T(1024)S(1)}, f32[1024]{0:T(1024)}, u32[]{:S(2)}) copy-start(f32[1024]{0:T(1024)} %get-tuple-element.116) | copy-start | bytes 12292
  258.0 51.6 %copy-start.38 = (f32[1024]{0:T(1024)S(1)}, f32[1024]{0:T(1024)}, u32[]{:S(2)}) copy-start(f32[1024]{0:T(1024)} %get-tuple-element.118) | copy-start | bytes 12292
  258.0 52.2 %copy-start.32 = (f32[1024]{0:T(1024)S(1)}, f32[1024]{0:T(1024)}, u32[]{:S(2)}) copy-start(f32[1024]{0:T(1024)} %get-tuple-element.93) | copy-start | bytes 12292
  259.5 53.2 %copy-start.52 = (s32[128]{0:T(128)S(1)}, s32[128]{0:T(128)}, u32[]{:S(2)}) copy-start(s32[128]{0:T(128)} %convert_reduce_fusion.2) | copy-start | bytes 1540
  264.4 50.7 %all-to-all-start.6 = ((bf16[128,8,256]{2,0,1:T(8,128)(2,1)}), bf16[128,8,256]{2,0,1:T(8,128)(2,1)}, u32[]{:S(2)}, u32[]{:S(2)}) async-start(bf16[128,8,256]{2,0,1:T(8,128)(2,1)} %bitcast.104), calls=%async_computation.6 | async-start | bytes 1048576 | tf_op jit(solution)/shard_map/all_to_all | solution.py:315
  269.9 52.6 %copy-start.2 = (f32[128,2048]{1,0:T(8,128)S(1)}, f32[128,2048]{1,0:T(8,128)}, u32[]{:S(2)}) copy-start(f32[128,2048]{1,0:T(8,128)} %all-reduce.16.cloned.1.call-done) | copy-start | bytes 3145732
  269.9 52.6 %copy-start.40 = (f32[128]{0:T(128)S(1)}, f32[128]{0:T(128)}, u32[]{:S(2)}) copy-start(f32[128]{0:T(128)} %copy-done.39) | copy-start | bytes 1540
  269.9 52.6 %copy-start.42 = (f32[128]{0:T(128)S(1)}, f32[128]{0:T(128)}, u32[]{:S(2)}) copy-start(f32[128]{0:T(128)} %copy-done.41) | copy-start | bytes 1540
  270.0 52.5 %copy-start.50 = (f32[128]{0:T(128)S(1)}, f32[128]{0:T(128)}, u32[]{:S(2)}) copy-start(f32[128]{0:T(128)} %copy-done.49) | copy-start | bytes 1540
  315.1 29.9 %copy-start.31 = (f32[1024]{0:T(1024)S(1)}, f32[1024]{0:T(1024)}, u32[]{:S(2)}) copy-start(f32[1024]{0:T(1024)} %get-tuple-element.99) | copy-start | bytes 12292
  315.1 31.1 %copy-start.48 = (f32[1024]{0:T(1024)S(1)}, f32[1024]{0:T(1024)}, u32[]{:S(2)}) copy-start(f32[1024]{0:T(1024)} %get-tuple-element.97) | copy-start | bytes 12292
  315.1 26.2 %all-to-all-start.1 = ((bf16[8,16,2048]{2,1,0:T(8,128)(2,1)}), bf16[8,16,2048]{2,1,0:T(8,128)(2,1)}, u32[]{:S(2)}, u32[]{:S(2)}) async-start(bf16[8,16,2048]{2,1,0:T(8,128)(2,1)} %bitcast.121), calls=%async_computation.1 | async-start | bytes 1048576 | tf_op jit(solution)/shard_map/all_to_all | solution.py:312
  325.5 51.4 %copy-start.55 = (s32[128]{0:T(128)S(1)}, s32[128]{0:T(128)}, u32[]{:S(2)}) copy-start(s32[128]{0:T(128)} %param.21) | copy-start | bytes 1540
  325.5 51.6 %copy-start.5 = (bf16[128,2048]{1,0:T(8,128)(2,1)S(1)}, bf16[128,2048]{1,0:T(8,128)(2,1)}, u32[]{:S(2)}) copy-start(bf16[128,2048]{1,0:T(8,128)(2,1)} %copy-done.4) | copy-start | bytes 1572868
  325.5 52.4 %copy-start.11 = (bf16[128,1024]{1,0:T(8,128)(2,1)S(1)}, bf16[128,1024]{1,0:T(8,128)(2,1)}, u32[]{:S(2)}) copy-start(bf16[128,1024]{1,0:T(8,128)(2,1)} %copy-done.10) | copy-start | bytes 786436
  325.5 52.4 %copy-start.19 = (bf16[128,1024]{1,0:T(8,128)(2,1)S(1)}, bf16[128,1024]{1,0:T(8,128)(2,1)}, u32[]{:S(2)}) copy-start(bf16[128,1024]{1,0:T(8,128)(2,1)} %get-tuple-element.114) | copy-start | bytes 786436
  341.3 31.9 %all-to-all-start.3 = ((bf16[8,16,2048]{2,1,0:T(8,128)(2,1)}), bf16[8,16,2048]{2,1,0:T(8,128)(2,1)S(1)}, u32[]{:S(2)}, u32[]{:S(2)}) async-start(bf16[8,16,2048]{2,1,0:T(8,128)(2,1)} %bitcast.116), calls=%async_computation.3 | async-start | bytes 1048576 | tf_op jit(solution)/shard_map/all_to_all | solution.py:312
  373.2 51.2 %all-to-all-start.4 = ((f32[8,1,40320]{2,1,0:T(1,128)}), f32[8,1,40320]{2,1,0:T(1,128)S(1)}, u32[]{:S(2)}, u32[]{:S(2)}) async-start(f32[8,1,40320]{2,1,0:T(1,128)} %copy.66), calls=%async_computation.4 | async-start | bytes 2580480 | tf_op jit(solution)/shard_map/all_to_all | solution.py:312
  376.8 246.8 %all-gather.5.cloned.1.call-start = ((), (), s32[]{:S(2)}) async-start(), calls=%async_computation.10 | async-start | bytes 4718592 | tf_op jit(solution)/shard_map/all_gather | solution.py:318
  424.4 205.6 %all-to-all-start.5 = ((bf16[128,8,256]{2,0,1:T(8,128)(2,1)}), bf16[128,8,256]{2,0,1:T(8,128)(2,1)S(1)}, u32[]{:S(2)}, u32[]{:S(2)}) async-start(bf16[128,8,256]{2,0,1:T(8,128)(2,1)} %bitcast.105), calls=%async_computation.5 | async-start | bytes 1048576 | tf_op jit(solution)/shard_map/all_to_all | solution.py:315
  (24 other events, 89.4 us)
Sparse Core Ops, SparseCore 0:
  46.0 31.0 all-reduce.11
  97.3 37.5 all-reduce.13
  166.7 36.4 all-reduce.15
  255.8 51.5 all-reduce.17
  309.4 65.4 all-gather.6
  376.9 98.3 all-gather.10
  477.4 72.3 all-gather.8
  551.9 71.6 all-gather.4
